TPU v7x, 256 devices: a whole 4x4x8 slice. The times are simulated.
256 devices in a mesh: shift: 8 (over x, core), rows: 32 (over y, z).
Axes of the slice: x: 4, y: 4, z: 8, core: 2. Of those that a mesh axis runs over, the one named last changes fastest.
Arguments:
- neighbours: int32 [256, 8], P('rows'), may hold values from 0 to 255, as said below
- couplings: float32 [256, 8, 128, 128], P('rows'), may hold values from -0.01953125 to 0.01953125
- eigvectors: float32 [256, 128, 128], P('rows'), may hold values from -1 to 1, as said below
- eigvalues: float32 [256, 128], P('rows'), may hold values from -2.5 to 2.5
- start_block: float32 [32768, 128], P('rows'), may hold values from -240 to 240
Outputs:
- basis: float32 [32768, 128], P('rows')
- basis_image: float32 [32768, 128], P('rows')
- projected: float32 [128, 128], replicated
Inputs may be any that keep to these rules, and one draw needn't show every extreme that they name: Each block's 8 neighbours are distinct blocks other than itself, each within 8 blocks of it. `eigvectors`: each block's matrix has orthonormal columns up to rounding.
All inputs are finite; a program needn't handle non-finite values.
Results may differ from a plain program's by a relative error of at most 0.00025.
Values sent between devices are 32-bit elements; how exact they have to be, the bound alone decides.
A program may use at most 64 MiB of HBM per device.

v0:
```python
import jax
import jax.numpy as jnp
from jax import lax
from jax.sharding import PartitionSpec as P

SWEEPS = 3


radius = 1.0
damping = 0.8


def extended(block, sides, width):
    for axis, dim in sides:
        count = lax.axis_size(axis)
        forward = [(i, i + 1) for i in range(count - 1)]
        backward = [(target, source) for source, target in forward]
        low = lax.ppermute(
            lax.slice_in_dim(block, block.shape[dim] - width, None, axis=dim), axis, forward
        )
        high = lax.ppermute(lax.slice_in_dim(block, 0, width, axis=dim), axis, backward)
        block = jnp.concatenate([low, block, high], axis=dim)
    return block


def unrotate(vectors, field):
    return jnp.einsum("imn,imc->inc", vectors, field, precision=lax.Precision.HIGHEST)


def rotate(vectors, field):
    return jnp.einsum("inm,imc->inc", vectors, field, precision=lax.Precision.HIGHEST)


def shifted_inverse(vectors, values, field, real_part, imag_part):
    width = field.shape[-1] // 2
    spun = unrotate(vectors, field)
    offset = real_part - values
    denom = offset * offset + imag_part * imag_part
    scale_re = (offset / denom)[..., None]
    scale_im = (-imag_part / denom)[..., None]
    first = spun[..., :width]
    second = spun[..., width:]
    mixed = jnp.concatenate(
        [scale_re * first - scale_im * second, scale_re * second + scale_im * first], axis=-1
    )
    return rotate(vectors, mixed)


def diagonal_part(vectors, values, field):
    return rotate(vectors, values[..., None] * unrotate(vectors, field))


def coupled(near_blocks, couplings):
    return jnp.einsum("iknm,ikmc->inc", couplings, near_blocks, precision=lax.Precision.HIGHEST)


def product(left, right):
    return jnp.dot(left, right, precision=lax.Precision.HIGHEST)


def per_device(neighbours, couplings, eigvectors, eigvalues, start_block):
    blk_dev, blk = eigvalues.shape
    ncol = start_block.shape[1]
    rows_here = blk_dev * blk
    total = rows_here * lax.axis_size("rows")
    count = lax.axis_size("shift")
    angle = jnp.pi * (lax.axis_index("shift").astype(jnp.float32) + 0.5) / count
    real_part = radius * jnp.cos(angle)
    imag_part = radius * jnp.sin(angle)
    local_index = neighbours - (lax.axis_index("rows") * blk_dev - blk_dev)

    def operate_on(field, padded):
        blocks_all = padded.reshape(3 * blk_dev, blk, padded.shape[-1])
        near = blocks_all[local_index]
        return diagonal_part(eigvectors, eigvalues, field) + coupled(near, couplings)

    blocks_b = start_block.reshape(blk_dev, blk, ncol)
    rhs = jnp.concatenate([blocks_b, jnp.zeros_like(blocks_b)], axis=-1)
    iterate = damping * shifted_inverse(eigvectors, eigvalues, rhs, real_part, imag_part)
    for sweep in range(1, SWEEPS):
        first = iterate[..., :ncol]
        second = iterate[..., ncol:]
        shifted = jnp.concatenate(
            [real_part * first - imag_part * second, imag_part * first + real_part * second],
            axis=-1,
        )
        iterate_padded = extended(iterate.reshape(rows_here, 2 * ncol), (("rows", 0),), rows_here)
        resid = rhs - shifted + operate_on(iterate, iterate_padded)
        iterate = iterate + damping * shifted_inverse(
            eigvectors, eigvalues, resid, real_part, imag_part
        )
    contrib = real_part / count * iterate[..., :ncol] - imag_part / count * iterate[..., ncol:]
    contrib = contrib.reshape(rows_here, ncol)
    field = lax.psum(contrib, "shift")
    gram = lax.psum(product(field.T, field), "rows") / total
    factor = jnp.linalg.cholesky(gram)
    basis = jax.scipy.linalg.solve_triangular(factor, field.T, lower=True).T
    padded = extended(basis, (("rows", 0),), rows_here)
    image = operate_on(basis.reshape(blk_dev, blk, ncol), padded).reshape(rows_here, ncol)
    projected = lax.psum(product(basis.T, image), "rows") / total
    basis_image, projected = (image, projected)
    return (basis, basis_image, projected)


def solution(mesh):
    in_specs = (
        P("rows", None),
        P("rows", None, None, None),
        P("rows", None, None),
        P("rows", None),
        P("rows", None),
    )
    out_specs = (P("rows", None), P("rows", None), P())
    return jax.shard_map(
        per_device, mesh=mesh, in_specs=in_specs, out_specs=out_specs, check_vma=False
    )
```

profile of v0, /device:TPU:1, one launch (start us, length us, event | category | flops | bytes accessed | tf_op | source)
XLA Modules:
  0.0 552.3 jit_solution(6460307151305128019)
XLA Ops:
  12.9 5.4 collective-permute-start
  22.9 16.5 %collective-permute-done = f32[1024,256]{1,0:T(8,128)} collective-permute-done((f32[1024,256]{1,0:T(8,128)}, f32[1024,256]{1,0:T(8,128)}, u32[]{:S(2)}, u32[]{:S(2)}) %collective-permute-start) | collective-permute-done | bytes 1048608 | tf_op jit(solution)/shard_map/ppermute | solution.py:18
  39.4 4.8 collective-permute-done.1
  44.2 3.8 pad_maximum_fusion
  48.0 6.2 %gather_fusion = f32[64,128,256]{2,1,0:T(8,128)} fusion(f32[24,128,256]{2,1,0:T(8,128)} %bitcast.105, s32[1024]{0:T(1024)S(1)} %pad_clamp_fusion), kind=kCustom, calls=%fused_computation | custom fusion | bytes 16777472 | tf_op jit(solution)/shard_map/gather | solution.py:74
  54.2 17.3 %fusion.11 = f32[8,128,256]{1,2,0:T(8,128)S(1)} fusion(f32[8,256,128]{2,1,0:T(8,128)S(1)} %fusion.37, f32[8,8,128,256]{3,2,1,0:T(8,128)} %bitcast.108, f32[8,8,128,128]{3,2,1,0:T(8,128)} %param.6, f32[8,128,128]{1,2,0:T(8,128)S(1)} %copy.20, f32[8,128,128]{1,2,0:T(8,128)} %get-tuple-element.18, f32[8,128,128]{1,2,0:T(8,128)} %get-tuple-element.17), kind=kOutput, calls=%fused_computation.26 | convolution fusion | flops 3222274048 | bytes 16252928 | tf_op jit(solution)/shard_map/iknm,ikmc->inc/dot_general | solution.py:54
  75.1 3.9 collective-permute-start.2
  83.6 15.7 %collective-permute-done.2 = f32[1024,256]{1,0:T(8,128)} collective-permute-done((f32[1024,256]{1,0:T(8,128)}, f32[1024,256]{1,0:T(8,128)}, u32[]{:S(2)}, u32[]{:S(2)}) %collective-permute-start.2) | collective-permute-done | bytes 1048608 | tf_op jit(solution)/shard_map/ppermute | solution.py:18
  99.2 5.7 %collective-permute-done.3 = f32[1024,256]{1,0:T(8,128)} collective-permute-done((f32[1024,256]{1,0:T(8,128)}, f32[1024,256]{1,0:T(8,128)}, u32[]{:S(2)}, u32[]{:S(2)}) %collective-permute-start.3) | collective-permute-done | bytes 1048608 | tf_op jit(solution)/shard_map/ppermute | solution.py:21
  105.0 3.8 pad_maximum_fusion.1
  108.7 6.2 %gather_fusion.1 = f32[64,128,256]{2,1,0:T(8,128)} fusion(f32[24,128,256]{2,1,0:T(8,128)} %bitcast.106, s32[1024]{0:T(1024)S(1)} %pad_clamp_fusion), kind=kCustom, calls=%fused_computation.1 | custom fusion | bytes 16777472 | tf_op jit(solution)/shard_map/gather | solution.py:74
  114.9 17.4 %fusion.14 = f32[8,128,256]{1,2,0:T(8,128)S(1)} fusion(f32[8,256,128]{2,1,0:T(8,128)S(1)} %fusion.38, f32[8,8,128,256]{3,2,1,0:T(8,128)} %bitcast.107, f32[8,8,128,128]{3,2,1,0:T(8,128)} %param.6, f32[8,128,128]{1,2,0:T(8,128)S(1)} %copy.20, f32[8,128,128]{1,2,0:T(8,128)} %get-tuple-element.16, f32[8,128,128]{1,2,0:T(8,128)} %get-tuple-element.15), kind=kOutput, calls=%fused_computation.29 | convolution fusion | flops 3222274048 | bytes 16252928 | tf_op jit(solution)/shard_map/iknm,ikmc->inc/dot_general | solution.py:54
  135.8 66.8 %all-reduce.5.cloned.1.call-done = f32[1024,128]{1,0:T(8,128)} async-done(((f32[1024,128]{1,0:T(8,128)}), f32[1024,128]{1,0:T(8,128)}) %all-reduce.5.cloned.1.call-update) | async-done | bytes 524304 | tf_op jit(solution)/shard_map/psum | solution.py:94
  202.6 2.8 fusion.39
  205.9 139.1 %all-reduce.7.cloned.1.call-done = f32[128,128]{0,1:T(8,128)} async-done(((f32[128,128]{0,1:T(8,128)}), f32[128,128]{0,1:T(8,128)}) %all-reduce.7.cloned.1.call-update) | async-done | bytes 65552 | tf_op jit(solution)/shard_map/psum | solution.py:95
  346.8 11.7 %cholesky.16 = f32[128,128]{1,0:T(8,128)S(1)} custom-call(f32[128,128]{1,0:T(8,128)S(1)} %fusion.30), custom_call_target="Cholesky" | custom-call | tf_op jit(solution)/shard_map/jit(cholesky)/cholesky | solution.py:96
  359.9 9.8 %custom-call.7 = f32[1,128,128]{1,2,0:T(8,128)S(1)} custom-call(f32[1,128,128]{2,1,0:T(8,128)S(1)} %fusion.27), custom_call_target="InvertDiagBlocksLowerTriangular" | custom-call | tf_op jit(solution)/shard_map/jit(_solve_triangular)/triangular_solve | solution.py:97
  371.4 3.0 collective-permute-start.4
  376.5 4.2 collective-permute-done.4
  380.7 3.6 collective-permute-done.5
  385.6 1.9 copy.48
  387.5 2.8 gather_fusion.2
  390.2 8.1 %convolution_bitcast_fusion.4 = f32[8,128,128]{1,2,0:T(8,128)S(1)} fusion(f32[8,8,128,128]{3,2,1,0:T(8,128)} %bitcast.112, f32[8,8,128,128]{3,2,1,0:T(8,128)} %param.6), kind=kOutput, calls=%fused_computation.30 | convolution fusion | flops 1610612736 | bytes 8912896 | tf_op jit(solution)/shard_map/iknm,ikmc->inc/dot_general | solution.py:54
  402.2 141.9 %all-reduce.9.cloned.1.call-done = f32[128,128]{0,1:T(8,128)} async-done(((f32[128,128]{0,1:T(8,128)}), f32[128,128]{0,1:T(8,128)}) %all-reduce.9.cloned.1.call-update) | async-done | bytes 65552 | tf_op jit(solution)/shard_map/psum | solution.py:100
  (55 shorter events, 35.7 us)
Async XLA Ops:
  7.2 1.5 copy-start
  7.2 195.4 %all-reduce.5.cloned.1.call-start = ((), (), s32[]{:S(2)}) async-start(), calls=%async_computation | async-start | bytes 1048576 | tf_op jit(solution)/shard_map/psum | solution.py:94
  8.6 10.9 %copy-start.3 = (s32[8,8]{1,0:T(8,128)S(1)}, s32[8,8]{1,0:T(8,128)}, u32[]{:S(2)}) copy-start(s32[8,8]{1,0:T(8,128)} %param.5) | copy-start | bytes 772
  10.3 10.4 %copy-start.2 = (f32[8,128]{1,0:T(8,128)S(1)}, f32[8,128]{1,0:T(8,128)}, u32[]{:S(2)}) copy-start(f32[8,128]{1,0:T(8,128)} %param.8) | copy-start | bytes 12292
  12.9 26.5 %collective-permute-start = (f32[1024,256]{1,0:T(8,128)}, f32[1024,256]{1,0:T(8,128)}, u32[]{:S(2)}, u32[]{:S(2)}) collective-permute-start(f32[1024,256]{1,0:T(8,128)} %bitcast.3), channel_id=1, source_target_pairs={{0,1},{1,2},{2,3},{3,4},{4,5},{5,6},{6,7},{7,8},{8,9},{9,10},{10,1... | collective-permute-start | bytes 3145736 | tf_op jit(solution)/shard_map/ppermute | solution.py:18
  18.2 26.0 %collective-permute-start.1 = (f32[1024,256]{1,0:T(8,128)}, f32[1024,256]{1,0:T(8,128)}, u32[]{:S(2)}, u32[]{:S(2)}) collective-permute-start(f32[1024,256]{1,0:T(8,128)} %bitcast.3), channel_id=1, source_target_pairs={{1,0},{2,1},{3,2},{4,3},{5,4},{6,5},{7,6},{8,7},{9,8},{10,9},{11,1... | collective-permute-start | bytes 3145736 | tf_op jit(solution)/shard_map/ppermute | solution.py:21
  75.1 24.1 %collective-permute-start.2 = (f32[1024,256]{1,0:T(8,128)}, f32[1024,256]{1,0:T(8,128)}, u32[]{:S(2)}, u32[]{:S(2)}) collective-permute-start(f32[1024,256]{1,0:T(8,128)} %bitcast.11), channel_id=1, source_target_pairs={{0,1},{1,2},{2,3},{3,4},{4,5},{5,6},{6,7},{7,8},{8,9},{9,10},{10,1... | collective-permute-start | bytes 3145736 | tf_op jit(solution)/shard_map/ppermute | solution.py:18
  79.0 25.9 %collective-permute-start.3 = (f32[1024,256]{1,0:T(8,128)}, f32[1024,256]{1,0:T(8,128)}, u32[]{:S(2)}, u32[]{:S(2)}) collective-permute-start(f32[1024,256]{1,0:T(8,128)} %bitcast.11), channel_id=1, source_target_pairs={{1,0},{2,1},{3,2},{4,3},{5,4},{6,5},{7,6},{8,7},{9,8},{10,9},{11,1... | collective-permute-start | bytes 3145736 | tf_op jit(solution)/shard_map/ppermute | solution.py:21
  135.7 209.3 %all-reduce.7.cloned.1.call-start = ((), (), s32[]{:S(2)}) async-start(), calls=%async_computation.1 | async-start | bytes 131072 | tf_op jit(solution)/shard_map/psum | solution.py:95
  205.5 338.6 %all-reduce.9.cloned.1.call-start = ((), (), s32[]{:S(2)}) async-start(), calls=%async_computation.2 | async-start | bytes 131072 | tf_op jit(solution)/shard_map/psum | solution.py:100
  371.4 9.3 %collective-permute-start.4 = (f32[1024,128]{0,1:T(8,128)S(1)}, f32[1024,128]{0,1:T(8,128)S(1)}, u32[]{:S(2)}, u32[]{:S(2)}) collective-permute-start(f32[1024,128]{0,1:T(8,128)S(1)} %bitcast.113), channel_id=1, source_target_pairs={{0,1},{1,2},{2,3},{3,4},{4,5},{5,6},{6,7},{7,8},{8,9},{9,10},{10,1... | collective-permute-start | bytes 1572872 | tf_op jit(solution)/shard_map/ppermute | solution.py:18
  374.4 9.9 %collective-permute-start.5 = (f32[1024,128]{0,1:T(8,128)S(1)}, f32[1024,128]{0,1:T(8,128)S(1)}, u32[]{:S(2)}, u32[]{:S(2)}) collective-permute-start(f32[1024,128]{0,1:T(8,128)S(1)} %bitcast.114), channel_id=1, source_target_pairs={{1,0},{2,1},{3,2},{4,3},{5,4},{6,5},{7,6},{8,7},{9,8},{10,9},{11,1... | collective-permute-start | bytes 1572872 | tf_op jit(solution)/shard_map/ppermute | solution.py:21
  399.5 146.1 %copy-start.1 = (f32[8,128,128]{1,2,0:T(8,128)}, f32[8,128,128]{1,2,0:T(8,128)S(1)}, u32[]{:S(2)}) copy-start(f32[8,128,128]{1,2,0:T(8,128)S(1)} %convolution_add_fusion) | copy-start | bytes 1572868
Sparse Core Ops, SparseCore 0:
  135.9 66.7 all-reduce.4
  206.6 138.3 all-reduce.6
  401.3 142.6 all-reduce.8
where the time goes:
time: 561 us; the launch traced here: 552 us
  waiting for transfers between devices  398 us (71%)
  matrix products  61.4 us (11%)
  other arithmetic  37.6 us (7%)
  local copies, waits for them, and re-layouts  23.8 us (4%)
  starting transfers between devices  16.8 us (3%)
  between operations  14.4 us (3%)
    psum x1, waiting for transfers between devices, per_device(): projected = lax.psum(product(basis.T, image), 'rows') / total  142 us
    psum x1, waiting for transfers between devices, per_device(): gram = lax.psum(product(field.T, field), 'rows') / total  139 us
    psum x1, waiting for transfers between devices, per_device(): field = lax.psum(contrib, 'shift')  66.8 us
    dot_general x3, matrix products, coupled(): jnp.einsum('iknm,ikmc->inc', couplings, near_blocks, precision=lax.Precis...  42.7 us
    ppermute x3, waiting for transfers between devices, extended(): lax.ppermute(lax.slice_in_dim(block, block.shape[dim] - width, None, axis...  36.4 us
    gather x3, local copies, waits for them, and re-layouts, operate_on(): near = blocks_all[local_index]  15.2 us
    ppermute x3, waiting for transfers between devices, extended(): lax.ppermute(lax.slice_in_dim(block, 0, width, axis=dim), axis, backward)  14.1 us
    another operation x3, other arithmetic, per_device(): factor = jnp.linalg.cholesky(gram)  12.4 us
  transfers between devices with their start and end apart: 9, of which 9 were waited for; matrix products, arithmetic and copies ran while one was open for 1% of the time, Pallas kernels for 0%

commit v1 on v0

v1 whole, which is shorter than its diff:
```python
import functools

import jax
import jax.numpy as jnp
import numpy as np
from jax import lax
from jax.experimental import pallas as pl
from jax.experimental.pallas import tpu as pltpu
from jax.sharding import PartitionSpec as P

MESH = pl.DeviceIdType.MESH
F32 = jnp.float32
BF16 = jnp.bfloat16
BD = 8
N = 128
NN = ((1,), (0,))
NT = ((1,), (1,))
RADIUS = 1.0
DAMPING = 0.8


def split(x):
    hi = x.astype(BF16)
    return hi, (x - hi.astype(F32)).astype(BF16)


def mm(a, b, dims=NN):
    return lax.dot_general(a, b, (dims, ((), ())), preferred_element_type=F32)


def mm3(a, b, dims=NN):
    return mm(a[0], b[0], dims) + (mm(a[0], b[1], dims) + mm(a[1], b[0], dims))


def exact(a, b, dims=NN):
    return lax.dot_general(
        a, b, (dims, ((), ())), precision=lax.Precision.HIGHEST, preferred_element_type=F32
    )


def main_kernel(
    S, R, Z,
    nbr, c_hbm, q_hbm, e_hbm, b_hbm, consts,
    f_out, af_out, g_out,
    cv, c2s, qp, ep, bv, bp, qs, qt, xh, xl, x2, xh2, xl2, y2, dr, di, bt, ft, fh, fa, afs, afa,
    zb, yb, gb,
    csem, qsem, esem, bsem, osem,
    q_s, q_r, qf_s, qf_r, e_s, e_r, b_s, b_r, x_s, x_r, f_s, f_r,
    ga_s, ga_r, gp_s, gp_r, ha_s, ha_r, hp_s, hp_r,
    z_s, z_r, y_s, y_r, g_s, g_r,
):
    W = N // S
    s = lax.axis_index("shift")
    r = lax.axis_index("rows")
    Y = R // Z
    yy, zz = r // Z, r % Z
    core = s % 2
    partner = s + 1 - 2 * core
    up, down = (r + 1) % R, (r + R - 1) % R
    X = S // 2
    xx = s // 2

    load_q = pltpu.make_async_copy(q_hbm, qp.at[pl.ds(BD, BD)], qsem)
    load_q.start()
    load_b = pltpu.make_async_copy(b_hbm, bv, bsem)
    load_b.start()
    load_e = pltpu.make_async_copy(e_hbm, ep.at[1], esem)
    load_e.start()
    load_c = pltpu.make_async_copy(c_hbm, cv, csem)
    load_c.start()

    barrier = pltpu.get_barrier_semaphore()

    def greet(where):
        pl.semaphore_signal(barrier, inc=1, device_id=where, device_id_type=MESH)

    greet({"rows": up})
    greet({"rows": down})
    for k in range(1, Z):
        greet({"rows": yy * Z + (zz + k) % Z})
    for k in range(1, Y):
        greet({"rows": ((yy + k) % Y) * Z + zz})
    for k in range(1, S):
        greet({"shift": (s + k) % S})
    pl.semaphore_wait(barrier, 2 + (Z - 1) + (Y - 1) + (S - 1))

    def remote(src, dst, ss, rs, where):
        return pltpu.make_async_remote_copy(
            src_ref=src, dst_ref=dst, send_sem=ss, recv_sem=rs,
            device_id=where, device_id_type=MESH,
        )

    HB = BD // 2
    q_up = remote(q_hbm.at[pl.ds(core * HB, HB)], qp.at[pl.ds(core * HB, HB)],
                  q_s.at[0], q_r.at[0], {"rows": up})
    q_dn = remote(q_hbm.at[pl.ds(core * HB, HB)], qp.at[pl.ds(2 * BD + core * HB, HB)],
                  q_s.at[1], q_r.at[1], {"rows": down})
    q_up.start()
    q_dn.start()
    e_up = remote(e_hbm, ep.at[0], e_s.at[0], e_r.at[0], {"rows": up})
    e_dn = remote(e_hbm, ep.at[2], e_s.at[1], e_r.at[1], {"rows": down})
    e_up.start()
    e_dn.start()

    lane = lax.broadcasted_iota(jnp.int32, (W, N), 1)
    row = lax.broadcasted_iota(jnp.int32, (W, N), 0)
    pick = (lane == row + s * W).astype(BF16)
    fold = (lane % W == row).astype(BF16)

    load_q.wait()
    load_b.wait()
    load_e.wait()

    def own_rhs(i, _):
        q = qp[BD + i]
        qh, ql = split(q)
        qs[0, i] = qh
        qs[1, i] = ql
        th, tl = split(q.T)
        qt[0, i] = th
        qt[1, i] = tl
        blk = bv[pl.ds(pl.multiple_of(i * N, N), N), :]
        bh = blk.astype(BF16)
        rest = blk - bh.astype(F32)
        bl = rest.astype(BF16)
        bm = (rest - bl.astype(F32)).astype(BF16)
        own = mm(pick, bh, NT) + (mm(pick, bl, NT) + mm(pick, bm, NT))
        bp[BD + i] = mm3(split(own), (qh, ql))
        return 0

    lax.fori_loop(0, BD, own_rhs, 0)

    b_up = remote(bp.at[pl.ds(BD, BD)], bp.at[pl.ds(0, BD)], b_s.at[0], b_r.at[0], {"rows": up})
    b_dn = remote(bp.at[pl.ds(BD, BD)], bp.at[pl.ds(2 * BD, BD)], b_s.at[1], b_r.at[1], {"rows": down})
    b_up.start()
    b_dn.start()

    za = consts[0:1, :]
    zbm = consts[1:2, :]
    wr = consts[2:3, :]
    wi = consts[3:4, :]

    def coefficients(e_row):
        offset = za - jnp.broadcast_to(e_row, (N, N)).T
        scale = DAMPING / (offset * offset + zbm * zbm)
        return offset * scale, -zbm * scale

    def spread(rhs):
        return jnp.concatenate([rhs] * S, axis=0).T

    def first(g, slot, qpair):
        c_re, c_im = coefficients(g)
        tile = spread(bp[slot])
        mixed = jnp.concatenate([c_re * tile, c_im * tile], axis=1)
        xv = mm3(qpair, split(mixed))
        h, l = split(xv)
        xh[slot] = h
        xl[slot] = l
        return c_re, c_im, tile, mixed

    def own_first(i, _):
        c_re, c_im, tile, mixed = first(ep[1, pl.ds(i, 1), :], BD + i, (qs[0, i], qs[1, i]))
        dr[i] = c_re
        di[i] = c_im
        bt[i] = tile
        y2[i] = mixed
        return 0

    lax.fori_loop(0, BD, own_first, 0)

    load_c.wait()

    def split_c(i, _):
        for k in range(BD):
            h, l = split(cv[i, k])
            c2s[i, 0:N, k * N:(k + 1) * N] = h
            c2s[i, N:2 * N, k * N:(k + 1) * N] = l
        return 0

    lax.fori_loop(0, BD, split_c, 0)

    q_up.wait_recv()
    qf_lo = remote(qp.at[pl.ds(core * HB, HB)], qp.at[pl.ds(core * HB, HB)],
                   qf_s.at[0], qf_r.at[0], {"shift": partner})
    qf_lo.start()
    q_dn.wait_recv()
    qf_hi = remote(qp.at[pl.ds(2 * BD + core * HB, HB)], qp.at[pl.ds(2 * BD + core * HB, HB)],
                   qf_s.at[1], qf_r.at[1], {"shift": partner})
    qf_hi.start()
    e_up.wait_recv()
    e_dn.wait_recv()
    b_up.wait_recv()
    b_dn.wait_recv()
    qf_lo.wait_recv()
    qf_hi.wait_recv()

    def halo_first(i, _):
        first(ep[0, pl.ds(i, 1), :], i, split(qp[i]))
        first(ep[2, pl.ds(i, 1), :], 2 * BD + i, split(qp[2 * BD + i]))
        return 0

    lax.fori_loop(0, BD, halo_first, 0)

    base = r * BD - BD

    def place(i, k):
        return jnp.clip(nbr[i, k] - base, 0, 3 * BD - 1)

    def coupled(i, hi_ref, lo_ref):
        acc = jnp.zeros((N, 2 * N), F32)
        for k in range(0, BD, 2):
            i0 = place(i, k)
            i1 = place(i, k + 1)
            hi = jnp.concatenate([hi_ref[i0], hi_ref[i1]], axis=0)
            lo = jnp.concatenate([lo_ref[i0], lo_ref[i1]], axis=0)
            both = mm(c2s[i, :, k * N:(k + 2) * N], hi)
            acc = acc + both[:N] + both[N:] + mm(c2s[i, :N, k * N:(k + 2) * N], lo)
        return acc

    def relaxed(i, hi_ref, lo_ref):
        spun = mm3((qt[0, i], qt[1, i]), split(coupled(i, hi_ref, lo_ref)))
        t_re = bt[i] + spun[:, :N]
        t_im = spun[:, N:]
        c_re, c_im = dr[i], di[i]
        old = y2[i]
        return (
            (1.0 - DAMPING) * old[:, :N] + (c_re * t_re - c_im * t_im),
            (1.0 - DAMPING) * old[:, N:] + (c_re * t_im + c_im * t_re),
        )

    def x_copies(i):
        return (
            remote(x2.at[BD + i], x2.at[i], x_s.at[0, i], x_r.at[0, i], {"rows": up}),
            remote(x2.at[BD + i], x2.at[2 * BD + i], x_s.at[1, i], x_r.at[1, i], {"rows": down}),
        )

    def sweep_one(i, _):
        re, im = relaxed(i, xh, xl)
        mixed = jnp.concatenate([re, im], axis=1)
        y2[i] = mixed
        xv = mm3((qs[0, i], qs[1, i]), split(mixed))
        x2[BD + i] = xv
        to_up, to_dn = x_copies(i)
        to_up.start()
        to_dn.start()
        h, l = split(xv)
        xh2[BD + i] = h
        xl2[BD + i] = l
        return 0

    lax.fori_loop(0, BD, sweep_one, 0)

    def arrive(i, _):
        to_up, to_dn = x_copies(i)
        to_up.wait_recv()
        h, l = split(x2[i])
        xh2[i] = h
        xl2[i] = l
        to_dn.wait_recv()
        h, l = split(x2[2 * BD + i])
        xh2[2 * BD + i] = h
        xl2[2 * BD + i] = l
        return 0

    lax.fori_loop(0, BD, arrive, 0)

    def sweep_two(i, _):
        re, im = relaxed(i, xh2, xl2)
        t = wr * re - wi * im
        t0 = t.astype(BF16)
        rest = t - t0.astype(F32)
        t1 = rest.astype(BF16)
        t2 = (rest - t1.astype(F32)).astype(BF16)
        hat = mm(fold, t0, NT) + (mm(fold, t1, NT) + mm(fold, t2, NT))
        fh[i] = hat
        ft[BD + i] = mm3(split(hat), (qs[0, i], qs[1, i]), NT)
        return 0

    lax.fori_loop(0, BD, sweep_two, 0)

    f_up = remote(ft.at[pl.ds(BD, BD)], ft.at[pl.ds(0, BD)], f_s.at[0], f_r.at[0], {"rows": up})
    f_dn = remote(ft.at[pl.ds(BD, BD)], ft.at[pl.ds(2 * BD, BD)], f_s.at[1], f_r.at[1], {"rows": down})
    f_up.start()
    f_dn.start()

    def gather_start(src, dst, ssem, rsem, psem, prsem):
        cross = []
        for k in range(1, X):
            c = remote(src, dst.at[s], ssem.at[k], rsem.at[k], {"shift": ((xx + k) % X) * 2 + core})
            c.start()
            cross.append(c)
        mine = remote(src, dst.at[s], psem.at[0], prsem.at[0], {"shift": partner})
        mine.start()
        return cross, mine

    def gather_forward(dst, cross, psem, prsem):
        on = []
        for k in range(1, X):
            cross[k - 1].wait_recv()
            origin = ((xx + X - k) % X) * 2 + core
            c = remote(dst.at[origin], dst.at[origin], psem.at[k], prsem.at[k], {"shift": partner})
            c.start()
            on.append(c)
        return on

    def gather_end(mine, on):
        mine.wait_recv()
        for c in on:
            c.wait_recv()

    f_cross, f_mine = gather_start(ft.at[pl.ds(BD, BD)], fa, ga_s, ga_r, gp_s, gp_r)
    fa[s] = ft[pl.ds(BD, BD)]
    f_up.wait_recv()
    f_dn.wait_recv()

    def image(i, _):
        acc = mm3(split(fh[i] * ep[1, pl.ds(i, 1), :]), (qs[0, i], qs[1, i]), NT)
        for k in range(0, BD, 2):
            i0 = place(i, k)
            i1 = place(i, k + 1)
            near = jnp.concatenate([ft[i0], ft[i1]], axis=1)
            h, l = split(near)
            ch = c2s[i, :N, k * N:(k + 2) * N]
            cl = c2s[i, N:, k * N:(k + 2) * N]
            acc = acc + mm3((h, l), (ch, cl), NT)
        afs[i] = acc
        return 0

    lax.fori_loop(0, BD, image, 0)

    f_on = gather_forward(fa, f_cross, gp_s, gp_r)
    h_cross, h_mine = gather_start(afs, afa, ha_s, ha_r, hp_s, hp_r)
    afa[s] = afs[...]
    gather_end(f_mine, f_on)
    out_f = pltpu.make_async_copy(fa, f_out, osem.at[0])
    out_f.start()

    def grams(i, acc):
        left = jnp.concatenate([ft[BD + i], afs[i]], axis=0)
        right = jnp.concatenate([fa[t, i] for t in range(S)], axis=0)
        return acc + exact(left, right, NT)

    zb[zz] = lax.fori_loop(0, BD, grams, jnp.zeros((2 * W, N), F32))

    z_cp = []
    for k in range(1, Z):
        c = remote(zb.at[zz], zb.at[zz], z_s.at[k], z_r.at[k], {"rows": yy * Z + (zz + k) % Z})
        c.start()
        z_cp.append(c)
    h_on = gather_forward(afa, h_cross, hp_s, hp_r)
    for c in z_cp:
        c.wait_recv()
    yb[yy] = functools.reduce(lambda a, t: a + zb[t], range(1, Z), zb[0])
    y_cp = []
    for k in range(1, Y):
        c = remote(yb.at[yy], yb.at[yy], y_s.at[k], y_r.at[k], {"rows": ((yy + k) % Y) * Z + zz})
        c.start()
        y_cp.append(c)
    for c in y_cp:
        c.wait_recv()
    gb[s] = functools.reduce(lambda a, t: a + yb[t], range(1, Y), yb[0])
    g_cp = []
    for k in range(1, S):
        c = remote(gb.at[s], gb.at[s], g_s.at[k], g_r.at[k], {"shift": (s + k) % S})
        c.start()
        g_cp.append(c)
    gather_end(h_mine, h_on)
    out_h = pltpu.make_async_copy(afa, af_out, osem.at[1])
    out_h.start()
    for c in g_cp:
        c.wait_recv()
    out_g = pltpu.make_async_copy(gb, g_out, osem.at[2])
    out_g.start()

    for c in (q_up, q_dn, e_up, e_dn, b_up, b_dn, qf_lo, qf_hi, f_up, f_dn):
        c.wait_send()
    for c in f_cross + [f_mine] + f_on + h_cross + [h_mine] + h_on + z_cp + y_cp + g_cp:
        c.wait_send()

    def sent(i, _):
        to_up, to_dn = x_copies(i)
        to_up.wait_send()
        to_dn.wait_send()
        return 0

    lax.fori_loop(0, BD, sent, 0)
    out_f.wait()
    out_h.wait()
    out_g.wait()


def inverse_factor(g):
    T, B = N // 8, 32
    sub = lax.broadcasted_iota(jnp.int32, (8, N), 0)
    lane = lax.broadcasted_iota(jnp.int32, (8, N), 1)
    a = [g[8 * t:8 * t + 8] for t in range(T)]
    m = [(lane == sub + 8 * t).astype(F32) for t in range(T)]
    for p in range(N // B):
        last = (p + 1) * B // 8
        for k in range(p * B, (p + 1) * B):
            t0, r0 = k // 8, k % 8
            head = jnp.broadcast_to(a[t0][:, k:k + 1], (8, N))
            inv = lax.rsqrt(jnp.broadcast_to(head[r0:r0 + 1, :], (8, N)))
            ra = jnp.broadcast_to(a[t0][r0:r0 + 1, :], (8, N)) * inv
            rm = jnp.broadcast_to(m[t0][r0:r0 + 1, :], (8, N)) * inv
            f = jnp.where(sub > r0, head * inv, 0.0)
            a[t0] = jnp.where(sub == r0, ra, a[t0] - f * ra)
            m[t0] = jnp.where(sub == r0, rm, m[t0] - f * rm)
            for t in range(t0 + 1, last):
                f = jnp.broadcast_to(a[t][:, k:k + 1], (8, N)) * inv
                a[t] = a[t] - f * ra
                m[t] = m[t] - f * rm
        if last < T:
            pa = jnp.concatenate(a[p * B // 8:last], axis=0)
            pm = jnp.concatenate(m[p * B // 8:last], axis=0)
            lower = pa.T[(p + 1) * B:, :]
            change = exact(lower, jnp.concatenate([pa, pm], axis=1))
            for t in range(last, T):
                part = change[8 * (t - last):8 * (t - last) + 8]
                a[t] = a[t] - part[:, :N]
                m[t] = m[t] - part[:, N:]
    return jnp.concatenate(m, axis=0)


def finish_kernel(S, total, f, af, g, basis, image, projected):
    W = N // S
    gram = jnp.concatenate([g[t, 0:W] for t in range(S)], axis=0) * (1.0 / total)
    h_t = jnp.concatenate([g[t, W:2 * W] for t in range(S)], axis=0) * (1.0 / total)
    inv = inverse_factor(gram)
    projected[...] = exact(exact(inv, h_t, NT), inv, NT)
    mt = split(inv.T)

    def out(i, _):
        at = pl.ds(pl.multiple_of(i * N, N), N)
        fi = jnp.concatenate([f[t, i] for t in range(S)], axis=0).T
        basis[at, :] = mm3(split(fi), mt)
        ai = jnp.concatenate([af[t, i] for t in range(S)], axis=0).T
        image[at, :] = mm3(split(ai), mt)
        return 0

    lax.fori_loop(0, BD, out, 0)


def solution(mesh):
    S, R = mesh.shape["shift"], mesh.shape["rows"]
    Z = 8 if R % 32 == 0 else max(R // 2, 1)
    Y = R // Z
    W = N // S
    X = S // 2
    angle = np.pi * (np.repeat(np.arange(S), W) + 0.5) / S
    table = np.zeros((8, N), np.float32)
    table[0] = RADIUS * np.cos(angle)
    table[1] = RADIUS * np.sin(angle)
    table[2] = table[0] / S
    table[3] = table[1] / S
    dma = pltpu.SemaphoreType.DMA
    vmem = pltpu.VMEM
    any_spec = pl.BlockSpec(memory_space=pl.ANY)
    vm = pl.BlockSpec(memory_space=vmem)
    stack = jax.ShapeDtypeStruct((S, BD, W, N), F32)

    def per_device(neighbours, couplings, eigvectors, eigvalues, start_block):
        f, af, g = pl.pallas_call(
            functools.partial(main_kernel, S, R, Z),
            out_shape=(stack, stack, jax.ShapeDtypeStruct((S, 2 * W, N), F32)),
            in_specs=[pl.BlockSpec(memory_space=pltpu.SMEM)] + [any_spec] * 4 + [vm],
            out_specs=(any_spec, any_spec, any_spec),
            scratch_shapes=[
                vmem((BD, BD, N, N), F32),
                vmem((BD, 2 * N, BD * N), BF16),
                vmem((3 * BD, N, N), F32),
                vmem((3, BD, N), F32),
                vmem((BD * N, N), F32),
                vmem((3 * BD, W, N), F32),
                vmem((2, BD, N, N), BF16),
                vmem((2, BD, N, N), BF16),
                vmem((3 * BD, N, 2 * N), BF16),
                vmem((3 * BD, N, 2 * N), BF16),
                vmem((3 * BD, N, 2 * N), F32),
                vmem((3 * BD, N, 2 * N), BF16),
                vmem((3 * BD, N, 2 * N), BF16),
                vmem((BD, N, 2 * N), F32),
                vmem((BD, N, N), F32),
                vmem((BD, N, N), F32),
                vmem((BD, N, N), F32),
                vmem((3 * BD, W, N), F32),
                vmem((BD, W, N), F32),
                vmem((S, BD, W, N), F32),
                vmem((BD, W, N), F32),
                vmem((S, BD, W, N), F32),
                vmem((Z, 2 * W, N), F32),
                vmem((Y, 2 * W, N), F32),
                vmem((S, 2 * W, N), F32),
                dma, dma, dma, dma, dma((3,)),
                dma((2,)), dma((2,)), dma((2,)), dma((2,)),
                dma((2,)), dma((2,)), dma((2,)), dma((2,)),
                dma((2, BD)), dma((2, BD)), dma((2,)), dma((2,)),
                dma((X,)), dma((X,)), dma((X,)), dma((X,)),
                dma((X,)), dma((X,)), dma((X,)), dma((X,)),
                dma((Z,)), dma((Z,)), dma((Y,)), dma((Y,)), dma((S,)), dma((S,)),
            ],
            compiler_params=pltpu.CompilerParams(
                collective_id=0, has_side_effects=True
            ),
            name="filter",
        )(neighbours, couplings, eigvectors, eigvalues, start_block, jnp.asarray(table))
        rows_here = start_block.shape[0]
        return pl.pallas_call(
            functools.partial(finish_kernel, S, rows_here * R),
            out_shape=(
                jax.ShapeDtypeStruct((rows_here, N), F32),
                jax.ShapeDtypeStruct((rows_here, N), F32),
                jax.ShapeDtypeStruct((N, N), F32),
            ),
            in_specs=[vm, vm, vm],
            out_specs=(vm, vm, vm),
            name="finish",
        )(f, af, g)

    in_specs = (
        P("rows", None),
        P("rows", None, None, None),
        P("rows", None, None),
        P("rows", None),
        P("rows", None),
    )
    out_specs = (P("rows", None), P("rows", None), P())
    return jax.shard_map(
        per_device, mesh=mesh, in_specs=in_specs, out_specs=out_specs, check_vma=False
    )
```

time: 561 us -> 108 us (0.19); the launches traced: 552 us -> 108 us
  waiting for transfers between devices: 398 us -> 0 us
  Pallas kernels: 0 us -> 107 us
  matrix products: 61.4 us -> 0 us
  other arithmetic: 37.6 us -> 0 us
  local copies, waits for them, and re-layouts: 23.8 us -> 0 us
  starting transfers between devices: 16.8 us -> 0 us
  between operations: 14.4 us -> 0.64 us
    psum x3 -> x0, waiting for transfers between devices: 348 us -> none  [the longest x1 142 us: per_device(): projected = lax.psum(product(basis.T, image), 'rows') / total]
    pallas_call x0 -> x2, Pallas kernels: none -> 107 us  [the longest x1 85.5 us: per_device(): pl.pallas_call(functools.partial(main_kernel, S, R, Z), out_shape=(stack,...]
    dot_general x17 -> x0, matrix products: 59.7 us -> none  [the longest x3 42.7 us: coupled(): jnp.einsum('iknm,ikmc->inc', couplings, near_blocks, precision=lax.Precis...]
    ppermute x6 -> x0, waiting for transfers between devices: 50.5 us -> none  [the longest x3 36.4 us: extended(): lax.ppermute(lax.slice_in_dim(block, block.shape[dim] - width, None, axis...]
    another operation x5 -> x0, other arithmetic: 22.9 us -> none  [the longest x3 12.4 us: per_device(): factor = jnp.linalg.cholesky(gram)]
    ppermute x6 -> x0, starting transfers between devices: 16.3 us -> none  [the longest x3 12.3 us: extended(): lax.ppermute(lax.slice_in_dim(block, block.shape[dim] - width, None, axis...]
    gather x3 -> x0, local copies, waits for them, and re-layouts: 15.2 us -> none  [operate_on(): near = blocks_all[local_index]]
    concatenate x3 -> x0, other arithmetic: 8.82 us -> none  [extended(): block = jnp.concatenate([low, block, high], axis=dim)]
  transfers between devices with their start and end apart: 9 -> 0, of which waited for: 9 -> 0; matrix products, arithmetic and copies ran while one was open for 1% -> 0% of each run, Pallas kernels for 0% -> 0%
where the time goes in v1:
time: 108 us
  Pallas kernels  107 us (99%)
    pallas_call x1, Pallas kernels, per_device(): pl.pallas_call(functools.partial(main_kernel, S, R, Z), out_shape=(stack,...  85.5 us
    pallas_call x1, Pallas kernels, per_device(): pl.pallas_call(functools.partial(finish_kernel, S, rows_here * R), out_sh...  21.6 us

profile of v1, /device:TPU:1, one launch (start us, length us, event | category | flops | bytes accessed | tf_op | source)
XLA Modules:
  0.0 107.8 jit_solution(11505334264026908586)
XLA Ops:
  0.6 85.5 %filter.1 = (f32[8,8,16,128]{3,2,1,0:T(8,128)}, f32[8,8,16,128]{3,2,1,0:T(8,128)}, f32[8,32,128]{2,1,0:T(8,128)}) custom-call(s32[8,8]{1,0:T(8,128)} %nbr.1, f32[8,8,128,128]{3,2,1,0:T(8,128)} %c_hbm.1, f32[8,128,128]{2,1,0:T(8,128)} %q_hbm.1, f32[8,128]{1,0:T(8,128)} %e_hbm.1, f32[1024,128]{1,0:T(8,128)} %b_hbm.1, f32[8,128]{1,0:T(8,128)} %constant.2.clone.consts), custom_call_target="tpu_custom_call" | custom-call | tf_op jit(solution)/shard_map/filter/pallas_call | solution.py:463
  86.2 21.6 %finish.1 = (f32[1024,128]{1,0:T(8,128)}, f32[1024,128]{1,0:T(8,128)}, f32[128,128]{1,0:T(8,128)}) custom-call(f32[8,8,16,128]{3,2,1,0:T(8,128)} %get-tuple-element.6.f, f32[8,8,16,128]{3,2,1,0:T(8,128)} %get-tuple-element.7.af, f32[8,32,128]{2,1,0:T(8,128)} %get-tuple-element.8.g), custom_call_target="tpu_custom_call" | custom-call | tf_op jit(solution)/shard_map/finish/pallas_call | solution.py:508

commit v2 on v1

--- a/solution.py
+++ b/solution.py
@@ -43,7 +43,7 @@
     nbr, c_hbm, q_hbm, e_hbm, b_hbm, consts,
     f_out, af_out, g_out,
     cv, c2s, qp, ep, bv, bp, qs, qt, xh, xl, x2, xh2, xl2, y2, dr, di, bt, ft, fh, fa, afs, afa,
-    zb, yb, gb,
+    fu, au, zb, yb, gb,
     csem, qsem, esem, bsem, osem,
     q_s, q_r, qf_s, qf_r, e_s, e_r, b_s, b_r, x_s, x_r, f_s, f_r,
     ga_s, ga_r, gp_s, gp_r, ha_s, ha_r, hp_s, hp_r,
@@ -82,7 +82,6 @@
         greet({"rows": ((yy + k) % Y) * Z + zz})
     for k in range(1, S):
         greet({"shift": (s + k) % S})
-    pl.semaphore_wait(barrier, 2 + (Z - 1) + (Y - 1) + (S - 1))
 
     def remote(src, dst, ss, rs, where):
         return pltpu.make_async_remote_copy(
@@ -91,21 +90,28 @@
         )
 
     HB = BD // 2
-    q_up = remote(q_hbm.at[pl.ds(core * HB, HB)], qp.at[pl.ds(core * HB, HB)],
-                  q_s.at[0], q_r.at[0], {"rows": up})
-    q_dn = remote(q_hbm.at[pl.ds(core * HB, HB)], qp.at[pl.ds(2 * BD + core * HB, HB)],
-                  q_s.at[1], q_r.at[1], {"rows": down})
-    q_up.start()
-    q_dn.start()
+
+    def q_copies(i):
+        at = core * HB + i
+        return (
+            remote(q_hbm.at[at], qp.at[at], q_s.at[0, i], q_r.at[0, i], {"rows": up}),
+            remote(q_hbm.at[at], qp.at[2 * BD + at], q_s.at[1, i], q_r.at[1, i], {"rows": down}),
+        )
+
+    def q_forward(i):
+        at = core * HB + i
+        return (
+            remote(qp.at[at], qp.at[at], qf_s.at[0, i], qf_r.at[0, i], {"shift": partner}),
+            remote(qp.at[2 * BD + at], qp.at[2 * BD + at], qf_s.at[1, i], qf_r.at[1, i],
+                   {"shift": partner}),
+        )
+
     e_up = remote(e_hbm, ep.at[0], e_s.at[0], e_r.at[0], {"rows": up})
     e_dn = remote(e_hbm, ep.at[2], e_s.at[1], e_r.at[1], {"rows": down})
-    e_up.start()
-    e_dn.start()
 
     lane = lax.broadcasted_iota(jnp.int32, (W, N), 1)
     row = lax.broadcasted_iota(jnp.int32, (W, N), 0)
     pick = (lane == row + s * W).astype(BF16)
-    fold = (lane % W == row).astype(BF16)
 
     load_q.wait()
     load_b.wait()
@@ -128,12 +134,22 @@
         bp[BD + i] = mm3(split(own), (qh, ql))
         return 0
 
-    lax.fori_loop(0, BD, own_rhs, 0)
+    lax.fori_loop(0, BD, own_rhs, 0, unroll=4)
+    pl.semaphore_wait(barrier, 2 + (Z - 1) + (Y - 1) + (S - 1))
+    e_up.start()
+    e_dn.start()
 
     b_up = remote(bp.at[pl.ds(BD, BD)], bp.at[pl.ds(0, BD)], b_s.at[0], b_r.at[0], {"rows": up})
     b_dn = remote(bp.at[pl.ds(BD, BD)], bp.at[pl.ds(2 * BD, BD)], b_s.at[1], b_r.at[1], {"rows": down})
     b_up.start()
     b_dn.start()
+
+    def q_send(i, _):
+        for c in q_copies(i):
+            c.start()
+        return 0
+
+    lax.fori_loop(0, HB, q_send, 0)
 
     za = consts[0:1, :]
     zbm = consts[1:2, :]
@@ -166,7 +182,7 @@
         y2[i] = mixed
         return 0
 
-    lax.fori_loop(0, BD, own_first, 0)
+    lax.fori_loop(0, BD, own_first, 0, unroll=2)
 
     load_c.wait()
 
@@ -179,27 +195,31 @@
 
     lax.fori_loop(0, BD, split_c, 0)
 
-    q_up.wait_recv()
-    qf_lo = remote(qp.at[pl.ds(core * HB, HB)], qp.at[pl.ds(core * HB, HB)],
-                   qf_s.at[0], qf_r.at[0], {"shift": partner})
-    qf_lo.start()
-    q_dn.wait_recv()
-    qf_hi = remote(qp.at[pl.ds(2 * BD + core * HB, HB)], qp.at[pl.ds(2 * BD + core * HB, HB)],
-                   qf_s.at[1], qf_r.at[1], {"shift": partner})
-    qf_hi.start()
     e_up.wait_recv()
     e_dn.wait_recv()
     b_up.wait_recv()
     b_dn.wait_recv()
-    qf_lo.wait_recv()
-    qf_hi.wait_recv()
-
-    def halo_first(i, _):
+
+    def halo_first(i):
         first(ep[0, pl.ds(i, 1), :], i, split(qp[i]))
         first(ep[2, pl.ds(i, 1), :], 2 * BD + i, split(qp[2 * BD + i]))
-        return 0
-
-    lax.fori_loop(0, BD, halo_first, 0)
+
+    def direct(i, _):
+        for c, on in zip(q_copies(i), q_forward(i)):
+            c.wait_recv()
+            on.start()
+        halo_first(core * HB + i)
+        return 0
+
+    lax.fori_loop(0, HB, direct, 0)
+
+    def forwarded(i, _):
+        for on in q_forward(i):
+            on.wait_recv()
+        halo_first((1 - core) * HB + i)
+        return 0
+
+    lax.fori_loop(0, HB, forwarded, 0)
 
     base = r * BD - BD
 
@@ -217,8 +237,7 @@
             acc = acc + both[:N] + both[N:] + mm(c2s[i, :N, k * N:(k + 2) * N], lo)
         return acc
 
-    def relaxed(i, hi_ref, lo_ref):
-        spun = mm3((qt[0, i], qt[1, i]), split(coupled(i, hi_ref, lo_ref)))
+    def relaxed(i, spun):
         t_re = bt[i] + spun[:, :N]
         t_im = spun[:, N:]
         c_re, c_im = dr[i], di[i]
@@ -235,7 +254,7 @@
         )
 
     def sweep_one(i, _):
-        re, im = relaxed(i, xh, xl)
+        re, im = relaxed(i, mm3((qt[0, i], qt[1, i]), split(coupled(i, xh, xl))))
         mixed = jnp.concatenate([re, im], axis=1)
         y2[i] = mixed
         xv = mm3((qs[0, i], qs[1, i]), split(mixed))
@@ -264,19 +283,33 @@
 
     lax.fori_loop(0, BD, arrive, 0)
 
+    def couple_two(i, _):
+        h, l = split(coupled(i, xh2, xl2))
+        xh[i] = h
+        xl[i] = l
+        return 0
+
+    lax.fori_loop(0, BD, couple_two, 0, unroll=2)
+
     def sweep_two(i, _):
-        re, im = relaxed(i, xh2, xl2)
-        t = wr * re - wi * im
-        t0 = t.astype(BF16)
-        rest = t - t0.astype(F32)
-        t1 = rest.astype(BF16)
-        t2 = (rest - t1.astype(F32)).astype(BF16)
-        hat = mm(fold, t0, NT) + (mm(fold, t1, NT) + mm(fold, t2, NT))
+        re, im = relaxed(i, mm3((qt[0, i], qt[1, i]), (xh[i], xl[i])))
+        t = (wr * re - wi * im).T
+        hat = t[0:W]
+        for j in range(1, S):
+            hat = hat + t[j * W:(j + 1) * W]
         fh[i] = hat
-        ft[BD + i] = mm3(split(hat), (qs[0, i], qs[1, i]), NT)
-        return 0
-
-    lax.fori_loop(0, BD, sweep_two, 0)
+        return 0
+
+    lax.fori_loop(0, BD, sweep_two, 0, unroll=2)
+
+    def filtered(i, _):
+        hat = fh[i]
+        q = (qs[0, i], qs[1, i])
+        ft[BD + i] = mm3(split(hat), q, NT)
+        afs[i] = mm3(split(hat * ep[1, pl.ds(i, 1), :]), q, NT)
+        return 0
+
+    lax.fori_loop(0, BD, filtered, 0, unroll=4)
 
     f_up = remote(ft.at[pl.ds(BD, BD)], ft.at[pl.ds(0, BD)], f_s.at[0], f_r.at[0], {"rows": up})
     f_dn = remote(ft.at[pl.ds(BD, BD)], ft.at[pl.ds(2 * BD, BD)], f_s.at[1], f_r.at[1], {"rows": down})
@@ -314,39 +347,43 @@
     f_dn.wait_recv()
 
     def image(i, _):
-        acc = mm3(split(fh[i] * ep[1, pl.ds(i, 1), :]), (qs[0, i], qs[1, i]), NT)
+        acc = afs[i]
         for k in range(0, BD, 2):
-            i0 = place(i, k)
-            i1 = place(i, k + 1)
-            near = jnp.concatenate([ft[i0], ft[i1]], axis=1)
-            h, l = split(near)
-            ch = c2s[i, :N, k * N:(k + 2) * N]
-            cl = c2s[i, N:, k * N:(k + 2) * N]
-            acc = acc + mm3((h, l), (ch, cl), NT)
+            h, l = split(jnp.concatenate([ft[place(i, k)], ft[place(i, k + 1)]], axis=1))
+            at = slice(k * N, (k + 2) * N)
+            both = mm(jnp.concatenate([h, l], axis=0), c2s[i, :N, at], NT)
+            acc = acc + (both[:W] + (both[W:] + mm(h, c2s[i, N:, at], NT)))
         afs[i] = acc
         return 0
 
-    lax.fori_loop(0, BD, image, 0)
+    lax.fori_loop(0, BD, image, 0, unroll=2)
 
     f_on = gather_forward(fa, f_cross, gp_s, gp_r)
     h_cross, h_mine = gather_start(afs, afa, ha_s, ha_r, hp_s, hp_r)
     afa[s] = afs[...]
     gather_end(f_mine, f_on)
-    out_f = pltpu.make_async_copy(fa, f_out, osem.at[0])
-    out_f.start()
+
+    def upright(i, dst, stack):
+        h, l = split(jnp.concatenate([stack[t, i] for t in range(S)], axis=0).T)
+        both = jnp.concatenate([h, l], axis=1)
+        dst[pl.ds(pl.multiple_of(i * N, N), N), :] = both
+        return both
 
     def grams(i, acc):
-        left = jnp.concatenate([ft[BD + i], afs[i]], axis=0)
-        right = jnp.concatenate([fa[t, i] for t in range(S)], axis=0)
-        return acc + exact(left, right, NT)
-
-    zb[zz] = lax.fori_loop(0, BD, grams, jnp.zeros((2 * W, N), F32))
+        both = upright(i, fu, fa)
+        h, l = split(jnp.concatenate([ft[BD + i], afs[i]], axis=0))
+        wide = mm(h, both)
+        return acc + (wide[:, :N] + (wide[:, N:] + mm(l, both[:, :N])))
+
+    zb[zz] = lax.fori_loop(0, BD, grams, jnp.zeros((2 * W, N), F32), unroll=4)
 
     z_cp = []
     for k in range(1, Z):
         c = remote(zb.at[zz], zb.at[zz], z_s.at[k], z_r.at[k], {"rows": yy * Z + (zz + k) % Z})
         c.start()
         z_cp.append(c)
+    out_f = pltpu.make_async_copy(fu, f_out, osem.at[0])
+    out_f.start()
     h_on = gather_forward(afa, h_cross, hp_s, hp_r)
     for c in z_cp:
         c.wait_recv()
@@ -365,14 +402,20 @@
         c.start()
         g_cp.append(c)
     gather_end(h_mine, h_on)
-    out_h = pltpu.make_async_copy(afa, af_out, osem.at[1])
+
+    def af_upright(i, _):
+        upright(i, au, afa)
+        return 0
+
+    lax.fori_loop(0, BD, af_upright, 0, unroll=2)
+    out_h = pltpu.make_async_copy(au, af_out, osem.at[1])
     out_h.start()
     for c in g_cp:
         c.wait_recv()
     out_g = pltpu.make_async_copy(gb, g_out, osem.at[2])
     out_g.start()
 
-    for c in (q_up, q_dn, e_up, e_dn, b_up, b_dn, qf_lo, qf_hi, f_up, f_dn):
+    for c in (e_up, e_dn, b_up, b_dn, f_up, f_dn):
         c.wait_send()
     for c in f_cross + [f_mine] + f_on + h_cross + [h_mine] + h_on + z_cp + y_cp + g_cp:
         c.wait_send()
@@ -384,61 +427,98 @@
         return 0
 
     lax.fori_loop(0, BD, sent, 0)
+
+    def q_sent(i, _):
+        for c in q_copies(i) + q_forward(i):
+            c.wait_send()
+        return 0
+
+    lax.fori_loop(0, HB, q_sent, 0)
     out_f.wait()
     out_h.wait()
     out_g.wait()
 
 
 def inverse_factor(g):
-    T, B = N // 8, 32
+    T = N // 8
     sub = lax.broadcasted_iota(jnp.int32, (8, N), 0)
     lane = lax.broadcasted_iota(jnp.int32, (8, N), 1)
     a = [g[8 * t:8 * t + 8] for t in range(T)]
     m = [(lane == sub + 8 * t).astype(F32) for t in range(T)]
-    for p in range(N // B):
-        last = (p + 1) * B // 8
-        for k in range(p * B, (p + 1) * B):
-            t0, r0 = k // 8, k % 8
-            head = jnp.broadcast_to(a[t0][:, k:k + 1], (8, N))
-            inv = lax.rsqrt(jnp.broadcast_to(head[r0:r0 + 1, :], (8, N)))
-            ra = jnp.broadcast_to(a[t0][r0:r0 + 1, :], (8, N)) * inv
-            rm = jnp.broadcast_to(m[t0][r0:r0 + 1, :], (8, N)) * inv
-            f = jnp.where(sub > r0, head * inv, 0.0)
-            a[t0] = jnp.where(sub == r0, ra, a[t0] - f * ra)
-            m[t0] = jnp.where(sub == r0, rm, m[t0] - f * rm)
-            for t in range(t0 + 1, last):
-                f = jnp.broadcast_to(a[t][:, k:k + 1], (8, N)) * inv
-                a[t] = a[t] - f * ra
-                m[t] = m[t] - f * rm
-        if last < T:
-            pa = jnp.concatenate(a[p * B // 8:last], axis=0)
-            pm = jnp.concatenate(m[p * B // 8:last], axis=0)
-            lower = pa.T[(p + 1) * B:, :]
-            change = exact(lower, jnp.concatenate([pa, pm], axis=1))
-            for t in range(last, T):
-                part = change[8 * (t - last):8 * (t - last) + 8]
-                a[t] = a[t] - part[:, :N]
-                m[t] = m[t] - part[:, N:]
+
+    def full(x):
+        return jnp.broadcast_to(x, (8, N))
+
+    for t in range(T):
+        col = [full(a[t][:, 8 * t + j:8 * t + j + 1]) for j in range(8)]
+        e = {(i, j): full(col[j][i:i + 1, :]) for j in range(8) for i in range(j, 8)}
+        inv, low, ra, rm = [], {}, [], []
+        for k in range(8):
+            inv.append(lax.rsqrt(e[k, k]))
+            for i in range(k + 1, 8):
+                low[i, k] = e[i, k] * inv[k]
+            for j in range(k + 1, 8):
+                for i in range(j, 8):
+                    e[i, j] = e[i, j] - low[i, k] * low[j, k]
+            xa, xm = full(a[t][k:k + 1, :]), full(m[t][k:k + 1, :])
+            for j in range(k):
+                xa = xa - low[k, j] * ra[j]
+                xm = xm - low[k, j] * rm[j]
+            ra.append(xa * inv[k])
+            rm.append(xm * inv[k])
+        x = rm[0]
+        for k in range(1, 8):
+            x = jnp.where(sub == k, rm[k], x)
+        m[t] = x
+        for u in range(t + 1, T):
+            ls = []
+            for k in range(8):
+                y = full(a[u][:, 8 * t + k:8 * t + k + 1])
+                for j in range(k):
+                    y = y - ls[j] * low[k, j]
+                ls.append(y * inv[k])
+            for k in range(8):
+                a[u] = a[u] - ls[k] * ra[k]
+                m[u] = m[u] - ls[k] * rm[k]
     return jnp.concatenate(m, axis=0)
 
 
-def finish_kernel(S, total, f, af, g, basis, image, projected):
+def finish_kernel(S, total, f_hbm, af_hbm, g, basis, image, projected, fv, av, bv, iv, sem, osem):
     W = N // S
+    load_f = pltpu.make_async_copy(f_hbm, fv, sem.at[0])
+    load_f.start()
+    load_a = pltpu.make_async_copy(af_hbm, av, sem.at[1])
+    load_a.start()
     gram = jnp.concatenate([g[t, 0:W] for t in range(S)], axis=0) * (1.0 / total)
     h_t = jnp.concatenate([g[t, W:2 * W] for t in range(S)], axis=0) * (1.0 / total)
     inv = inverse_factor(gram)
-    projected[...] = exact(exact(inv, h_t, NT), inv, NT)
-    mt = split(inv.T)
+    mh, ml = split(inv.T)
+    twice = jnp.concatenate([mh, mh], axis=0)
+    load_f.wait()
+    load_a.wait()
+
+    def stores(i):
+        at = pl.ds(pl.multiple_of(i * N, N), N)
+        return (
+            pltpu.make_async_copy(bv.at[at, :], basis.at[at, :], osem.at[0, i]),
+            pltpu.make_async_copy(iv.at[at, :], image.at[at, :], osem.at[1, i]),
+        )
 
     def out(i, _):
         at = pl.ds(pl.multiple_of(i * N, N), N)
-        fi = jnp.concatenate([f[t, i] for t in range(S)], axis=0).T
-        basis[at, :] = mm3(split(fi), mt)
-        ai = jnp.concatenate([af[t, i] for t in range(S)], axis=0).T
-        image[at, :] = mm3(split(ai), mt)
-        return 0
-
-    lax.fori_loop(0, BD, out, 0)
+        fi = fv[at, :]
+        bv[at, :] = mm(fi, twice) + mm(fi[:, :N], ml)
+        ai = av[at, :]
+        iv[at, :] = mm(ai, twice) + mm(ai[:, :N], ml)
+        for c in stores(i):
+            c.start()
+        return 0
+
+    lax.fori_loop(0, BD, out, 0, unroll=4)
+    projected[...] = mm3(split(mm3(split(inv), split(h_t), NT)), (mh, ml))
+    for i in range(BD):
+        for c in stores(i):
+            c.wait()
 
 
 def solution(mesh):
@@ -457,7 +537,7 @@
     vmem = pltpu.VMEM
     any_spec = pl.BlockSpec(memory_space=pl.ANY)
     vm = pl.BlockSpec(memory_space=vmem)
-    stack = jax.ShapeDtypeStruct((S, BD, W, N), F32)
+    stack = jax.ShapeDtypeStruct((BD * N, 2 * N), BF16)
 
     def per_device(neighbours, couplings, eigvectors, eigvalues, start_block):
         f, af, g = pl.pallas_call(
@@ -488,11 +568,13 @@
                 vmem((S, BD, W, N), F32),
                 vmem((BD, W, N), F32),
                 vmem((S, BD, W, N), F32),
+                vmem((BD * N, 2 * N), BF16),
+                vmem((BD * N, 2 * N), BF16),
                 vmem((Z, 2 * W, N), F32),
                 vmem((Y, 2 * W, N), F32),
                 vmem((S, 2 * W, N), F32),
                 dma, dma, dma, dma, dma((3,)),
-                dma((2,)), dma((2,)), dma((2,)), dma((2,)),
+                dma((2, BD // 2)), dma((2, BD // 2)), dma((2, BD // 2)), dma((2, BD // 2)),
                 dma((2,)), dma((2,)), dma((2,)), dma((2,)),
                 dma((2, BD)), dma((2, BD)), dma((2,)), dma((2,)),
                 dma((X,)), dma((X,)), dma((X,)), dma((X,)),
@@ -512,8 +594,16 @@
                 jax.ShapeDtypeStruct((rows_here, N), F32),
                 jax.ShapeDtypeStruct((N, N), F32),
             ),
-            in_specs=[vm, vm, vm],
-            out_specs=(vm, vm, vm),
+            in_specs=[any_spec, any_spec, vm],
+            out_specs=(any_spec, any_spec, vm),
+            scratch_shapes=[
+                vmem((BD * N, 2 * N), BF16),
+                vmem((BD * N, 2 * N), BF16),
+                vmem((BD * N, N), F32),
+                vmem((BD * N, N), F32),
+                dma((2,)),
+                dma((2, BD)),
+            ],
             name="finish",
         )(f, af, g)
 

time: 108 us -> 84.9 us (0.79)
  Pallas kernels: 107 us -> 84.1 us
    pallas_call x1, Pallas kernels: 21.6 us -> 8.23 us  [per_device(): pl.pallas_call(functools.partial(finish_kernel, S, rows_here * R), out_sh...]
    pallas_call x1, Pallas kernels: 85.5 us -> 75.9 us  [per_device(): pl.pallas_call(functools.partial(main_kernel, S, R, Z), out_shape=(stack,...]
where the time goes in v2:
time: 84.9 us; the launch traced here: 84.7 us
  Pallas kernels  84.1 us (99%)
    pallas_call x1, Pallas kernels, per_device(): pl.pallas_call(functools.partial(main_kernel, S, R, Z), out_shape=(stack,...  75.9 us
    pallas_call x1, Pallas kernels, per_device(): pl.pallas_call(functools.partial(finish_kernel, S, rows_here * R), out_sh...  8.23 us

profile of v2, /device:TPU:1, one launch (start us, length us, event | category | flops | bytes accessed | tf_op | source)
XLA Modules:
  0.0 84.7 jit_solution(16527554555344490887)
XLA Ops:
  0.6 75.9 %filter.1 = (bf16[1024,256]{1,0:T(8,128)(2,1)}, bf16[1024,256]{1,0:T(8,128)(2,1)}, f32[8,32,128]{2,1,0:T(8,128)}) custom-call(s32[8,8]{1,0:T(8,128)} %nbr.1, f32[8,8,128,128]{3,2,1,0:T(8,128)} %c_hbm.1, f32[8,128,128]{2,1,0:T(8,128)} %q_hbm.1, f32[8,128]{1,0:T(8,128)} %e_hbm.1, f32[1024,128]{1,0:T(8,128)} %b_hbm.1, f32[8,128]{1,0:T(8,128)} %constant.2.clone.consts), custom_call_target="tpu_custom_call" | custom-call | tf_op jit(solution)/shard_map/filter/pallas_call | solution.py:543
  76.5 8.2 %finish.1 = (f32[1024,128]{1,0:T(8,128)}, f32[1024,128]{1,0:T(8,128)}, f32[128,128]{1,0:T(8,128)}) custom-call(bf16[1024,256]{1,0:T(8,128)(2,1)} %get-tuple-element.6.f_hbm, bf16[1024,256]{1,0:T(8,128)(2,1)} %get-tuple-element.7.af_hbm, f32[8,32,128]{2,1,0:T(8,128)} %get-tuple-element.8.g), custom_call_target="tpu_custom_call" | custom-call | tf_op jit(solution)/shard_map/finish/pallas_call | solution.py:590
